TPU v7x, 512 devices: a whole 4x8x8 slice. The times are simulated.
512 devices in a mesh: row: 32 (over y, z_lo), col: 16 (over z_hi, x, core).
Axes of the slice: x: 4, y: 8, z: 8 (z_hi: 2, z_lo: 4; z = z_hi * 4 + z_lo), core: 2. Of those that a mesh axis runs over, the one named last changes fastest.
Arguments:
- table: float32 [16, 256, 256], P('col', 'row'), may hold values from -4 to 4
- marginals: int32 [4096], replicated, may hold values from 64 to 4095
- visits: int32 [32, 16, 16], P('row', 'col'), may hold values from 0 to 15
- counts: int32 [32, 16, 16, 256, 256], P('row', 'col'), may hold values from 0 to 16, as said below
Outputs:
- gradient: float32 [16, 256, 256], P('col')
Inputs may be any that keep to these rules, and one draw needn't show every extreme that they name: `counts`: about half of the cells of every tile are zero.
All inputs are finite; a program needn't handle non-finite values.
Results may differ from a plain program's by a relative error of at most 0.0031.
Values may be sent and summed in bfloat16 or wider, within the bound.
A program may use at most 128 MiB of HBM per device.

v0:
```python
import jax
import jax.numpy as jnp
from jax import lax
from jax.sharding import PartitionSpec as P

K = 16
LOSS_SCALE = 0.0625


def from_root(value, axis, source):
    kept = jnp.where(lax.axis_index(axis) == source, value, 0).astype(value.dtype)
    return lax.psum(kept, axis)


def tile_terms(row_vectors, col_vectors, count_tile, log_rows, log_cols, log_total):
    logits = lax.dot_general(
        row_vectors, col_vectors, (((1,), (1,)), ((), ())), preferred_element_type=jnp.float32
    )
    count_vals = count_tile.astype(jnp.float32)
    baseline = log_total - log_rows[:, None] - log_cols[None, :]
    margin = logits - baseline
    fitted = (0.1 + 0.25 * jnp.sqrt(count_vals)) * (margin - jnp.log(jnp.maximum(count_vals, 1.0)))
    soft_hinge = jax.nn.sigmoid(margin)
    grad_logits = (jnp.where(count_vals > 0, fitted, soft_hinge) * LOSS_SCALE).astype(jnp.bfloat16)
    row_term = jnp.dot(grad_logits, col_vectors, preferred_element_type=jnp.float32)
    col_term = lax.dot_general(
        grad_logits, row_vectors, (((0,), (0,)), ((), ())), preferred_element_type=jnp.float32
    )
    return (row_term, col_term)


def local(table, marginals, visits, counts):
    blocks = lax.axis_size("col")
    row_devices = lax.axis_size("row")
    own_block = lax.axis_index("row") % blocks
    pieces = table.astype(jnp.bfloat16)
    block_rows = pieces.shape[1] * row_devices
    embed_width = pieces.shape[2]
    log_marg = jnp.log(marginals.astype(jnp.float32)).reshape(blocks, block_rows)
    log_total = jnp.log(jnp.sum(marginals).astype(jnp.float32))
    visited = visits[0, 0]
    count_tiles = counts[0, 0]
    log_rows = log_marg[own_block]
    zero_block = jnp.zeros((block_rows, embed_width), jnp.float32)
    col_block = lax.all_gather(pieces, "row", axis=1, tiled=True)
    row_vectors = from_root(col_block, "col", own_block)[0]
    start_terms = jnp.zeros((K, block_rows, embed_width), jnp.float32)
    shards = lax.all_gather(col_block, "col", axis=0, tiled=True)
    visit_row_sum = zero_block
    visit_col_terms = start_terms
    for k in range(K):
        visit_id = visited[k]
        inside = (visit_id >= 0) & (visit_id < shards.shape[0])
        col_vectors = lax.dynamic_index_in_dim(
            shards, jnp.clip(visit_id, 0, shards.shape[0] - 1), 0, keepdims=False
        )

        def compute(vectors, tile_k=count_tiles[k], log_cols=log_marg[visit_id]):
            return tile_terms(row_vectors, vectors, tile_k, log_rows, log_cols, log_total)

        def skipped(vectors):
            return (zero_block, zero_block)

        row_term, col_term = lax.cond(inside, compute, skipped, col_vectors)
        visit_row_sum = visit_row_sum + row_term
        visit_col_terms = visit_col_terms.at[k].add(col_term)
    block_ids = jnp.arange(1 * lax.axis_size("col"), dtype=jnp.int32)
    result = jnp.zeros((1 * lax.axis_size("col"), block_rows, embed_width), jnp.float32)
    for dense_k in range(K):
        result = result + jnp.where(
            (block_ids == visited[dense_k])[:, None, None], visit_col_terms[dense_k][None], 0.0
        )
    result = result + jnp.where((block_ids == own_block)[:, None, None], visit_row_sum[None], 0.0)
    summed = lax.psum_scatter(result, "col", scatter_dimension=0, tiled=True)
    return lax.psum(summed, "row")


def solution(mesh):
    return jax.shard_map(
        local,
        mesh=mesh,
        in_specs=(
            P("col", "row", None),
            P(),
            P("row", "col", None),
            P("row", "col", None, None, None),
        ),
        out_specs=P("col", None, None),
        check_vma=False,
    )
```

profile of v0, /device:TPU:2, one launch (start us, length us, event | category | flops | bytes accessed | tf_op | source)
XLA Modules:
  0.0 988.8 jit_solution(14721961554316318443)
XLA Ops:
  7.2 82.3 %all_gather.6 = bf16[1,256,256]{2,1,0:T(8,128)(2,1)S(1)} all-gather(bf16[1,8,256]{2,1,0:T(8,128)(2,1)S(1)} %convert_element_type.204), channel_id=1, replica_groups=mesh['row'=32,'col'=16] {'row'}, dimensions={1}, use_global_device_ids=true | all-gather | bytes 135168 | tf_op jit(solution)/shard_map/all_gather | solution.py:45
  91.1 2.0 fusion.207
  112.9 1.4 reduce_sum.9
  117.5 1.8 iota_compare_fusion.3
  119.4 1.8 iota_compare_fusion.5
  121.2 1.8 iota_compare_fusion.7
  123.0 1.7 iota_compare_fusion.9
  124.6 1.8 iota_compare_fusion.11
  126.4 1.8 iota_compare_fusion.13
  128.2 1.9 iota_compare_fusion.15
  130.1 135.8 %all-reduce.4.cloned.1.call-done = bf16[256,256]{1,0:T(8,128)(2,1)} async-done(((bf16[256,256]{1,0:T(8,128)(2,1)}), bf16[256,256]{1,0:T(8,128)(2,1)}) %all-reduce.4.cloned.1.call-update) | async-done | bytes 131088 | tf_op jit(solution)/shard_map/psum | solution.py:12
  265.9 79.2 %all-gather.2.cloned.1.call-done = bf16[16,256,256]{2,1,0:T(8,128)(2,1)} async-done(((bf16[1,256,256]{2,1,0:T(8,128)(2,1)}), bf16[16,256,256]{2,1,0:T(8,128)(2,1)}) %all-gather.2.cloned.1.call-update) | async-done | bytes 2097168 | tf_op jit(solution)/shard_map/all_gather | solution.py:48
  345.1 13.3 %conditional.16 = (f32[256,256]{1,0:T(8,128)S(1)}, f32[16,256,256]{2,1,0:T(8,128)}) conditional(s32[]{:T(128)} %convert_element_type.203, () %tuple.261, (s32[1,1,16,256,256]{4,3,2,1,0:T(8,128)}, s32[]{:T(128)}, bf16[16,256,256]{2,1,0:T(8,128)(2,1)}, bf16[256,256]{1,0:T(8,128)(2,1)}, f32[]{:T(128)}, /*index=5*/f32[1,256]{1,0:T(1,128)S(1)}, ...), branch_computations={%region_2.3_spmd, %region_3.4_spmd} | conditional | flops 101646592 | bytes 15079546 | solution.py:64
  347.8 5.4 copy.21
  353.2 1.4 fusion.4
  354.8 2.4 scatter-add.14
  358.4 10.6 %conditional.17 = (f32[256,256]{1,0:T(8,128)S(1)}, f32[1,256,256]{2,1,0:T(8,128)S(1)}) conditional(s32[]{:T(128)} %convert_element_type.207, () %tuple.263, (s32[1,1,16,256,256]{4,3,2,1,0:T(8,128)}, s32[]{:T(128)}, bf16[16,256,256]{2,1,0:T(8,128)(2,1)}, bf16[256,256]{1,0:T(8,128)(2,1)}, f32[]{:T(128)}, /*index=5*/f32[1,256]{1,0:T(1,128)S(1)}, ...), branch_computations={%region_4.5_spmd, %region_5.6_spmd} | conditional | flops 101646592 | bytes 10623094 | solution.py:64
  360.9 5.4 copy.22
  369.8 10.9 %conditional.18 = (f32[256,256]{1,0:T(8,128)S(1)}, f32[1,256,256]{2,1,0:T(8,128)S(1)}) conditional(s32[]{:T(128)} %convert_element_type.208, () %tuple.265, (s32[1,1,16,256,256]{4,3,2,1,0:T(8,128)}, s32[]{:T(128)}, bf16[16,256,256]{2,1,0:T(8,128)(2,1)}, bf16[256,256]{1,0:T(8,128)(2,1)}, f32[]{:T(128)}, /*index=5*/f32[1,256]{1,0:T(1,128)S(1)}, ...), branch_computations={%region_6.7_spmd, %region_7.8_spmd} | conditional | flops 101646592 | bytes 10623094 | solution.py:64
  372.5 5.4 copy.23
  380.7 1.7 fusion.204
  382.4 10.6 %conditional.19 = (f32[256,256]{1,0:T(8,128)S(1)}, f32[1,256,256]{2,1,0:T(8,128)S(1)}) conditional(s32[]{:T(128)} %convert_element_type.209, () %tuple.267, (s32[1,1,16,256,256]{4,3,2,1,0:T(8,128)}, s32[]{:T(128)}, bf16[16,256,256]{2,1,0:T(8,128)(2,1)}, bf16[256,256]{1,0:T(8,128)(2,1)}, f32[]{:T(128)}, /*index=5*/f32[1,256]{1,0:T(1,128)S(1)}, ...), branch_computations={%region_8.9_spmd, %region_9.10_spmd} | conditional | flops 101646592 | bytes 10623094 | solution.py:64
  384.9 5.4 copy.24
  393.0 1.7 fusion.203
  394.7 10.6 %conditional.20 = (f32[256,256]{1,0:T(8,128)S(1)}, f32[1,256,256]{2,1,0:T(8,128)S(1)}) conditional(s32[]{:T(128)} %convert_element_type.210, () %tuple.269, (s32[1,1,16,256,256]{4,3,2,1,0:T(8,128)}, s32[]{:T(128)}, bf16[16,256,256]{2,1,0:T(8,128)(2,1)}, bf16[256,256]{1,0:T(8,128)(2,1)}, f32[]{:T(128)}, /*index=5*/f32[1,256]{1,0:T(1,128)S(1)}, ...), branch_computations={%region_10.11_spmd, %region_11.12_spmd} | conditional | flops 101646592 | bytes 10623094 | solution.py:64
  397.2 5.4 copy.25
  405.3 1.7 fusion.202
  407.0 10.4 %conditional.21 = (f32[256,256]{1,0:T(8,128)S(1)}, f32[1,256,256]{2,1,0:T(8,128)S(1)}) conditional(s32[]{:T(128)} %convert_element_type.211, () %tuple.271, (s32[1,1,16,256,256]{4,3,2,1,0:T(8,128)}, s32[]{:T(128)}, bf16[16,256,256]{2,1,0:T(8,128)(2,1)}, bf16[256,256]{1,0:T(8,128)(2,1)}, f32[]{:T(128)}, /*index=5*/f32[1,256]{1,0:T(1,128)S(1)}, ...), branch_computations={%region_12.13_spmd, %region_13.14_spmd} | conditional | flops 101646592 | bytes 10623094 | solution.py:64
  409.3 5.4 copy.26
  417.4 1.7 fusion.201
  419.1 10.4 %conditional.22 = (f32[256,256]{1,0:T(8,128)S(1)}, f32[1,256,256]{2,1,0:T(8,128)S(1)}) conditional(s32[]{:T(128)} %convert_element_type.212, () %tuple.273, (s32[1,1,16,256,256]{4,3,2,1,0:T(8,128)}, s32[]{:T(128)}, bf16[16,256,256]{2,1,0:T(8,128)(2,1)}, bf16[256,256]{1,0:T(8,128)(2,1)}, f32[]{:T(128)}, /*index=5*/f32[1,256]{1,0:T(1,128)S(1)}, ...), branch_computations={%region_14.15_spmd, %region_15.16_spmd} | conditional | flops 101646592 | bytes 10623094 | solution.py:64
  421.4 5.4 copy.27
  429.5 1.7 fusion.200
  431.2 10.4 %conditional.23 = (f32[256,256]{1,0:T(8,128)S(1)}, f32[1,256,256]{2,1,0:T(8,128)S(1)}) conditional(s32[]{:T(128)} %convert_element_type.213, () %tuple.275, (s32[1,1,16,256,256]{4,3,2,1,0:T(8,128)}, s32[]{:T(128)}, bf16[16,256,256]{2,1,0:T(8,128)(2,1)}, bf16[256,256]{1,0:T(8,128)(2,1)}, f32[]{:T(128)}, /*index=5*/f32[1,256]{1,0:T(1,128)S(1)}, ...), branch_computations={%region_16.17_spmd, %region_17.18_spmd} | conditional | flops 101646592 | bytes 10623094 | solution.py:64
  433.5 5.4 copy.28
  441.6 1.7 fusion.199
  443.3 10.8 %conditional.24 = (f32[256,256]{1,0:T(8,128)S(1)}, f32[1,256,256]{2,1,0:T(8,128)S(1)}) conditional(s32[]{:T(128)} %convert_element_type.214, () %tuple.277, (s32[1,1,16,256,256]{4,3,2,1,0:T(8,128)}, s32[]{:T(128)}, bf16[16,256,256]{2,1,0:T(8,128)(2,1)}, bf16[256,256]{1,0:T(8,128)(2,1)}, f32[]{:T(128)}, /*index=5*/f32[1,256]{1,0:T(1,128)S(1)}, ...), branch_computations={%region_18.19_spmd, %region_19.20_spmd} | conditional | flops 101646592 | bytes 10623094 | solution.py:64
  446.0 5.4 copy.29
  454.1 1.7 fusion.198
  455.8 10.6 %conditional.25 = (f32[256,256]{1,0:T(8,128)S(1)}, f32[1,256,256]{2,1,0:T(8,128)S(1)}) conditional(s32[]{:T(128)} %convert_element_type.215, () %tuple.279, (s32[1,1,16,256,256]{4,3,2,1,0:T(8,128)}, s32[]{:T(128)}, bf16[16,256,256]{2,1,0:T(8,128)(2,1)}, bf16[256,256]{1,0:T(8,128)(2,1)}, f32[]{:T(128)}, /*index=5*/f32[1,256]{1,0:T(1,128)S(1)}, ...), branch_computations={%region_20.21_spmd, %region_21.22_spmd} | conditional | flops 101646592 | bytes 10623094 | solution.py:64
  458.3 5.4 copy.30
  466.4 1.7 fusion.197
  468.2 10.5 %conditional.26 = (f32[256,256]{1,0:T(8,128)S(1)}, f32[1,256,256]{2,1,0:T(8,128)S(1)}) conditional(s32[]{:T(128)} %convert_element_type.216, () %tuple.281, (s32[1,1,16,256,256]{4,3,2,1,0:T(8,128)}, s32[]{:T(128)}, bf16[16,256,256]{2,1,0:T(8,128)(2,1)}, bf16[256,256]{1,0:T(8,128)(2,1)}, f32[]{:T(128)}, /*index=5*/f32[1,256]{1,0:T(1,128)S(1)}, ...), branch_computations={%region_22.23_spmd, %region_23.24_spmd} | conditional | flops 101646592 | bytes 10623094 | solution.py:64
  470.5 5.4 copy.31
  478.6 1.7 fusion.196
  480.3 10.9 %conditional.27 = (f32[256,256]{1,0:T(8,128)S(1)}, f32[1,256,256]{2,1,0:T(8,128)S(1)}) conditional(s32[]{:T(128)} %convert_element_type.217, () %tuple.283, (s32[1,1,16,256,256]{4,3,2,1,0:T(8,128)}, s32[]{:T(128)}, bf16[16,256,256]{2,1,0:T(8,128)(2,1)}, bf16[256,256]{1,0:T(8,128)(2,1)}, f32[]{:T(128)}, /*index=5*/f32[1,256]{1,0:T(1,128)S(1)}, ...), branch_computations={%region_24.25_spmd, %region_25.26_spmd} | conditional | flops 101646592 | bytes 10623094 | solution.py:64
  483.1 5.4 copy.32
  491.3 1.7 fusion.195
  493.0 12.3 %conditional.28 = (f32[256,256]{1,0:T(8,128)S(1)}, f32[1,256,256]{2,1,0:T(8,128)}) conditional(s32[]{:T(128)} %convert_element_type.218, () %tuple.285, (s32[1,1,16,256,256]{4,3,2,1,0:T(8,128)}, s32[]{:T(128)}, bf16[16,256,256]{2,1,0:T(8,128)(2,1)}, bf16[256,256]{1,0:T(8,128)(2,1)}, f32[]{:T(128)}, /*index=5*/f32[1,256]{1,0:T(1,128)S(1)}, ...), branch_computations={%region_26.27_spmd, %region_27.28_spmd} | conditional | flops 101646592 | bytes 10623094 | solution.py:64
  496.4 5.4 copy.33
  505.3 1.9 fusion.205
  507.1 13.3 %conditional.29 = (f32[256,256]{1,0:T(8,128)}, f32[1,256,256]{2,1,0:T(8,128)}) conditional(s32[]{:T(128)} %convert_element_type.219, () %tuple.287, (s32[1,1,16,256,256]{4,3,2,1,0:T(8,128)}, s32[]{:T(128)}, bf16[16,256,256]{2,1,0:T(8,128)(2,1)}, bf16[256,256]{1,0:T(8,128)(2,1)}, f32[]{:T(128)}, /*index=5*/f32[1,256]{1,0:T(1,128)S(1)}, ...), branch_computations={%region_28.29_spmd, %region_29.30_spmd} | conditional | flops 101646592 | bytes 10623094 | solution.py:64
  511.0 5.4 copy.34
  518.6 1.8 fusion.161
  520.5 13.3 %conditional.30 = (f32[256,256]{1,0:T(8,128)}, f32[1,256,256]{2,1,0:T(8,128)}) conditional(s32[]{:T(128)} %convert_element_type.220, () %tuple.289, (s32[1,1,16,256,256]{4,3,2,1,0:T(8,128)}, s32[]{:T(128)}, bf16[16,256,256]{2,1,0:T(8,128)(2,1)}, bf16[256,256]{1,0:T(8,128)(2,1)}, f32[]{:T(128)}, /*index=5*/f32[1,256]{1,0:T(1,128)S(1)}, ...), branch_computations={%region_30.31_spmd, %region_31.32_spmd} | conditional | flops 101646592 | bytes 10623094 | solution.py:64
  524.3 5.4 copy.35
  531.9 1.9 fusion.173
  533.8 11.7 %conditional.31 = (f32[256,256]{1,0:T(8,128)S(1)}, f32[1,256,256]{2,1,0:T(8,128)S(1)}) conditional(s32[]{:T(128)} %convert_element_type.221, () %tuple.291, (s32[1,1,16,256,256]{4,3,2,1,0:T(8,128)}, s32[]{:T(128)}, bf16[16,256,256]{2,1,0:T(8,128)(2,1)}, bf16[256,256]{1,0:T(8,128)(2,1)}, f32[]{:T(128)}, /*index=5*/f32[1,256]{1,0:T(1,128)S(1)}, ...), branch_computations={%region_32.33_spmd, %region_33.34_spmd} | conditional | flops 101646592 | bytes 10627218 | solution.py:64
  537.4 5.4 copy.36
  546.3 2.8 slice_bitcast_fusion.11
  550.7 11.3 %select_add_fusion = f32[16,256,256]{2,1,0:T(8,128)} fusion(f32[256,256]{1,0:T(8,128)S(1)} %add_add_fusion, f32[256,256]{1,0:T(8,128)S(1)} %get-tuple-element.1640, f32[256,256]{1,0:T(8,128)S(1)} %get-tuple-element.1641, f32[256,256]{1,0:T(8,128)S(1)} %get-tuple-element.1642, f32[256,256]{1,0:T(8,128)S(1)} %copy-done.20, ...), kind=kLoop, calls=%fused_computation.288 | loop fusion | flops 34603008 | bytes 8651024 | tf_op jit(solution)/shard_map/add | solution.py:73
  562.1 109.4 %reduce-scatter.2.cloned.1.call-done = f32[1,256,256]{2,1,0:T(8,128)} async-done(((f32[16,256,256]{2,1,0:T(8,128)}), f32[1,256,256]{2,1,0:T(8,128)}) %reduce-scatter.2.cloned.1.call-update) | async-done | bytes 262160 | tf_op jit(solution)/shard_map/reduce_scatter | solution.py:74
  671.6 309.0 %all-reduce.6.cloned.1.call-done = f32[1,256,256]{2,1,0:T(8,128)} async-done(((f32[1,256,256]{2,1,0:T(8,128)}), f32[1,256,256]{2,1,0:T(8,128)}) %all-reduce.6.cloned.1.call-update) | async-done | bytes 262160 | tf_op jit(solution)/shard_map/psum | solution.py:75
  980.6 1.7 copy.115
  (152 shorter events, 53.6 us)
Async XLA Ops:
  6.5 259.4 %all-reduce.4.cloned.1.call-start = ((), (), s32[]{:S(2)}) async-start(), calls=%async_computation.2 | async-start | bytes 262144 | tf_op jit(solution)/shard_map/psum | solution.py:12
  89.5 0.8 copy-start.16
  90.3 254.8 %all-gather.2.cloned.1.call-start = ((), (), s32[]{:S(2)}) async-start(), calls=%async_computation.1 | async-start | bytes 2228224 | tf_op jit(solution)/shard_map/all_gather | solution.py:48
  91.0 580.5 %reduce-scatter.2.cloned.1.call-start = ((), (), s32[]{:S(2)}) async-start(), calls=%async_computation.3 | async-start | bytes 4456448 | tf_op jit(solution)/shard_map/reduce_scatter | solution.py:74
  115.1 365.3 %copy-start.21 = (f32[16,256]{1,0:T(8,128)}, f32[16,256]{1,0:T(8,128)S(1)}, u32[]{:S(2)}) copy-start(f32[16,256]{1,0:T(8,128)S(1)} %reshape.989) | copy-start | bytes 49156
  347.8 5.4 copy-start
  360.9 5.4 copy-start.1
  372.5 5.4 copy-start.2
  384.9 5.4 copy-start.3
  397.2 5.4 copy-start.4
  409.3 5.4 copy-start.5
  421.4 5.4 copy-start.6
  433.5 5.4 copy-start.7
  446.0 5.4 copy-start.8
  458.3 5.4 copy-start.9
  470.5 5.4 copy-start.10
  483.1 5.4 copy-start.11
  496.4 5.4 copy-start.12
  511.0 5.4 copy-start.13
  524.2 5.4 copy-start.14
  537.3 5.5 copy-start.15
  537.3 5.5 copy-start.35
  545.5 0.7 copy-start.17
  545.5 0.8 copy-start.19
  546.3 3.0 copy-start.18
  549.1 1.5 copy-start.20
  549.1 1.5 copy-start.22
  549.1 1.5 copy-start.23
  549.1 1.5 copy-start.24
  549.2 1.5 copy-start.25
  549.2 1.5 copy-start.26
  549.2 1.5 copy-start.27
  549.2 1.5 copy-start.28
  549.2 1.5 copy-start.29
  549.2 1.5 copy-start.30
  549.2 1.5 copy-start.31
  549.2 1.5 copy-start.32
  549.2 1.5 copy-start.33
  549.2 1.5 copy-start.34
  549.3 1.5 copy-start.36
  562.1 418.5 %all-reduce.6.cloned.1.call-start = ((), (), s32[]{:S(2)}) async-start(), calls=%async_computation.4 | async-start | bytes 524288 | tf_op jit(solution)/shard_map/psum | solution.py:75
Sparse Core Ops, SparseCore 0:
  90.4 175.4 all-reduce.3
  269.2 75.8 all-gather.1
  562.2 109.3 reduce-scatter.1
  674.3 306.2 all-reduce.5
where the time goes:
time: 992 us; the launch traced here: 989 us
  waiting for transfers between devices  634 us (64%)
  local copies, waits for them, and re-layouts  94.5 us (10%)
  blocking collectives  82.3 us (8%)
  other arithmetic  56.7 us (6%)
  matrix products  46.3 us (5%)
  loops' own time  40.4 us (4%)
  between operations  34.2 us (3%)
    psum x1, waiting for transfers between devices, local(): return lax.psum(summed, 'row')  309 us
    psum x1, waiting for transfers between devices, from_root(): return lax.psum(kept, axis)  136 us
    reduce_scatter x1, waiting for transfers between devices, local(): summed = lax.psum_scatter(result, 'col', scatter_dimension=0, tiled=True)  109 us
    another operation x16, local copies, waits for them, and re-layouts  86.8 us
    all_gather x1, blocking collectives, local(): col_block = lax.all_gather(pieces, 'row', axis=1, tiled=True)  82.3 us
    all_gather x1, waiting for transfers between devices, local(): shards = lax.all_gather(col_block, 'col', axis=0, tiled=True)  79.2 us
    another operation x16, loops' own time, local(): row_term, col_term = lax.cond(inside, compute, skipped, col_vectors)  40.4 us
    dot_general x16, matrix products, tile_terms(): lax.dot_general(row_vectors, col_vectors, (((1,), (1,)), ((), ())), prefe...  21.7 us
  transfers between devices with their start and end apart: 4, of which 4 were waited for; matrix products, arithmetic and copies ran while one was open for 2% of the time, Pallas kernels for 0%

commit v1 on v0

--- a/solution.py
+++ b/solution.py
@@ -30,6 +30,11 @@
 
 
 def local(table, marginals, visits, counts):
+
+    def _settle_axis_part(arr):
+        before = lax.all_gather(arr, "row").sum(axis=0)
+        return before
+
     blocks = lax.axis_size("col")
     row_devices = lax.axis_size("row")
     own_block = lax.axis_index("row") % blocks
@@ -72,7 +77,7 @@
         )
     result = result + jnp.where((block_ids == own_block)[:, None, None], visit_row_sum[None], 0.0)
     summed = lax.psum_scatter(result, "col", scatter_dimension=0, tiled=True)
-    return lax.psum(summed, "row")
+    return _settle_axis_part(summed)
 
 
 def solution(mesh):

time: 992 us -> 879 us (0.89)
  waiting for transfers between devices: 634 us -> 518 us
    psum x1 -> x0, waiting for transfers between devices: 309 us -> none  [local(): return lax.psum(summed, 'row')]
    all_gather x0 -> x1, waiting for transfers between devices: none -> 193 us  [_settle_axis_part(): before = lax.all_gather(arr, 'row').sum(axis=0)]
where the time goes in v1:
time: 879 us; the launch traced here: 876 us
  waiting for transfers between devices  518 us (59%)
  local copies, waits for them, and re-layouts  92.9 us (11%)
  blocking collectives  82.3 us (9%)
  other arithmetic  61.4 us (7%)
  matrix products  46.3 us (5%)
  loops' own time  40.4 us (5%)
  between operations  34.2 us (4%)
    all_gather x1, waiting for transfers between devices, _settle_axis_part(): before = lax.all_gather(arr, 'row').sum(axis=0)  193 us
    psum x1, waiting for transfers between devices, from_root(): return lax.psum(kept, axis)  136 us
    reduce_scatter x1, waiting for transfers between devices, local(): summed = lax.psum_scatter(result, 'col', scatter_dimension=0, tiled=True)  109 us
    another operation x16, local copies, waits for them, and re-layouts  86.8 us
    all_gather x1, blocking collectives, local(): col_block = lax.all_gather(pieces, 'row', axis=1, tiled=True)  82.3 us
    all_gather x1, waiting for transfers between devices, local(): shards = lax.all_gather(col_block, 'col', axis=0, tiled=True)  79.2 us
    another operation x16, loops' own time, local(): row_term, col_term = lax.cond(inside, compute, skipped, col_vectors)  40.4 us
    dot_general x16, matrix products, tile_terms(): lax.dot_general(row_vectors, col_vectors, (((1,), (1,)), ((), ())), prefe...  21.7 us
  transfers between devices with their start and end apart: 4, of which 4 were waited for; matrix products, arithmetic and copies ran while one was open for 2% of the time, Pallas kernels for 0%

profile of v1, /device:TPU:2, one launch (start us, length us, event | category | flops | bytes accessed | tf_op | source)
XLA Modules:
  0.0 875.6 jit_solution(2514432524063847271)
XLA Ops:
  7.2 82.3 %all_gather.12 = bf16[1,256,256]{2,1,0:T(8,128)(2,1)S(1)} all-gather(bf16[1,8,256]{2,1,0:T(8,128)(2,1)S(1)} %convert_element_type.204), channel_id=1, replica_groups=mesh['row'=32,'col'=16] {'row'}, dimensions={1}, use_global_device_ids=true | all-gather | bytes 135168 | tf_op jit(solution)/shard_map/all_gather | solution.py:50
  91.1 2.0 fusion.207
  112.9 1.4 reduce_sum.20
  117.5 1.8 iota_compare_fusion.3
  119.4 1.8 iota_compare_fusion.5
  121.2 1.8 iota_compare_fusion.7
  123.0 1.7 iota_compare_fusion.9
  124.6 1.8 iota_compare_fusion.11
  126.4 1.8 iota_compare_fusion.13
  128.2 1.9 iota_compare_fusion.15
  130.1 135.8 %all-reduce.3.cloned.1.call-done = bf16[256,256]{1,0:T(8,128)(2,1)} async-done(((bf16[256,256]{1,0:T(8,128)(2,1)}), bf16[256,256]{1,0:T(8,128)(2,1)}) %all-reduce.3.cloned.1.call-update) | async-done | bytes 131088 | tf_op jit(solution)/shard_map/psum | solution.py:12
  265.9 79.2 %all-gather.4.cloned.1.call-done = bf16[16,256,256]{2,1,0:T(8,128)(2,1)} async-done(((bf16[1,256,256]{2,1,0:T(8,128)(2,1)}), bf16[16,256,256]{2,1,0:T(8,128)(2,1)}) %all-gather.4.cloned.1.call-update) | async-done | bytes 2097168 | tf_op jit(solution)/shard_map/all_gather | solution.py:53
  345.1 13.3 %conditional.16 = (f32[256,256]{1,0:T(8,128)S(1)}, f32[16,256,256]{2,1,0:T(8,128)}) conditional(s32[]{:T(128)} %convert_element_type.203, () %tuple.261, (s32[1,1,16,256,256]{4,3,2,1,0:T(8,128)}, s32[]{:T(128)}, bf16[16,256,256]{2,1,0:T(8,128)(2,1)}, bf16[256,256]{1,0:T(8,128)(2,1)}, f32[]{:T(128)}, /*index=5*/f32[1,256]{1,0:T(1,128)S(1)}, ...), branch_computations={%region_2.3_spmd, %region_3.4_spmd} | conditional | flops 101646592 | bytes 15079546 | solution.py:69
  347.8 5.4 copy.21
  353.2 1.4 fusion.4
  354.8 2.4 scatter-add.14
  358.4 10.6 %conditional.17 = (f32[256,256]{1,0:T(8,128)S(1)}, f32[1,256,256]{2,1,0:T(8,128)S(1)}) conditional(s32[]{:T(128)} %convert_element_type.207, () %tuple.263, (s32[1,1,16,256,256]{4,3,2,1,0:T(8,128)}, s32[]{:T(128)}, bf16[16,256,256]{2,1,0:T(8,128)(2,1)}, bf16[256,256]{1,0:T(8,128)(2,1)}, f32[]{:T(128)}, /*index=5*/f32[1,256]{1,0:T(1,128)S(1)}, ...), branch_computations={%region_4.5_spmd, %region_5.6_spmd} | conditional | flops 101646592 | bytes 10623094 | solution.py:69
  360.9 5.4 copy.22
  369.8 10.9 %conditional.18 = (f32[256,256]{1,0:T(8,128)S(1)}, f32[1,256,256]{2,1,0:T(8,128)S(1)}) conditional(s32[]{:T(128)} %convert_element_type.208, () %tuple.265, (s32[1,1,16,256,256]{4,3,2,1,0:T(8,128)}, s32[]{:T(128)}, bf16[16,256,256]{2,1,0:T(8,128)(2,1)}, bf16[256,256]{1,0:T(8,128)(2,1)}, f32[]{:T(128)}, /*index=5*/f32[1,256]{1,0:T(1,128)S(1)}, ...), branch_computations={%region_6.7_spmd, %region_7.8_spmd} | conditional | flops 101646592 | bytes 10623094 | solution.py:69
  372.5 5.4 copy.23
  380.7 1.7 fusion.204
  382.4 10.6 %conditional.19 = (f32[256,256]{1,0:T(8,128)S(1)}, f32[1,256,256]{2,1,0:T(8,128)S(1)}) conditional(s32[]{:T(128)} %convert_element_type.209, () %tuple.267, (s32[1,1,16,256,256]{4,3,2,1,0:T(8,128)}, s32[]{:T(128)}, bf16[16,256,256]{2,1,0:T(8,128)(2,1)}, bf16[256,256]{1,0:T(8,128)(2,1)}, f32[]{:T(128)}, /*index=5*/f32[1,256]{1,0:T(1,128)S(1)}, ...), branch_computations={%region_8.9_spmd, %region_9.10_spmd} | conditional | flops 101646592 | bytes 10623094 | solution.py:69
  384.9 5.4 copy.24
  393.0 1.7 fusion.203
  394.7 10.6 %conditional.20 = (f32[256,256]{1,0:T(8,128)S(1)}, f32[1,256,256]{2,1,0:T(8,128)S(1)}) conditional(s32[]{:T(128)} %convert_element_type.210, () %tuple.269, (s32[1,1,16,256,256]{4,3,2,1,0:T(8,128)}, s32[]{:T(128)}, bf16[16,256,256]{2,1,0:T(8,128)(2,1)}, bf16[256,256]{1,0:T(8,128)(2,1)}, f32[]{:T(128)}, /*index=5*/f32[1,256]{1,0:T(1,128)S(1)}, ...), branch_computations={%region_10.11_spmd, %region_11.12_spmd} | conditional | flops 101646592 | bytes 10623094 | solution.py:69
  397.2 5.4 copy.25
  405.3 1.7 fusion.202
  407.0 10.4 %conditional.21 = (f32[256,256]{1,0:T(8,128)S(1)}, f32[1,256,256]{2,1,0:T(8,128)S(1)}) conditional(s32[]{:T(128)} %convert_element_type.211, () %tuple.271, (s32[1,1,16,256,256]{4,3,2,1,0:T(8,128)}, s32[]{:T(128)}, bf16[16,256,256]{2,1,0:T(8,128)(2,1)}, bf16[256,256]{1,0:T(8,128)(2,1)}, f32[]{:T(128)}, /*index=5*/f32[1,256]{1,0:T(1,128)S(1)}, ...), branch_computations={%region_12.13_spmd, %region_13.14_spmd} | conditional | flops 101646592 | bytes 10623094 | solution.py:69
  409.3 5.4 copy.26
  417.4 1.7 fusion.201
  419.1 10.4 %conditional.22 = (f32[256,256]{1,0:T(8,128)S(1)}, f32[1,256,256]{2,1,0:T(8,128)S(1)}) conditional(s32[]{:T(128)} %convert_element_type.212, () %tuple.273, (s32[1,1,16,256,256]{4,3,2,1,0:T(8,128)}, s32[]{:T(128)}, bf16[16,256,256]{2,1,0:T(8,128)(2,1)}, bf16[256,256]{1,0:T(8,128)(2,1)}, f32[]{:T(128)}, /*index=5*/f32[1,256]{1,0:T(1,128)S(1)}, ...), branch_computations={%region_14.15_spmd, %region_15.16_spmd} | conditional | flops 101646592 | bytes 10623094 | solution.py:69
  421.4 5.4 copy.27
  429.5 1.7 fusion.200
  431.2 10.4 %conditional.23 = (f32[256,256]{1,0:T(8,128)S(1)}, f32[1,256,256]{2,1,0:T(8,128)S(1)}) conditional(s32[]{:T(128)} %convert_element_type.213, () %tuple.275, (s32[1,1,16,256,256]{4,3,2,1,0:T(8,128)}, s32[]{:T(128)}, bf16[16,256,256]{2,1,0:T(8,128)(2,1)}, bf16[256,256]{1,0:T(8,128)(2,1)}, f32[]{:T(128)}, /*index=5*/f32[1,256]{1,0:T(1,128)S(1)}, ...), branch_computations={%region_16.17_spmd, %region_17.18_spmd} | conditional | flops 101646592 | bytes 10623094 | solution.py:69
  433.5 5.4 copy.28
  441.6 1.7 fusion.199
  443.3 10.8 %conditional.24 = (f32[256,256]{1,0:T(8,128)S(1)}, f32[1,256,256]{2,1,0:T(8,128)S(1)}) conditional(s32[]{:T(128)} %convert_element_type.214, () %tuple.277, (s32[1,1,16,256,256]{4,3,2,1,0:T(8,128)}, s32[]{:T(128)}, bf16[16,256,256]{2,1,0:T(8,128)(2,1)}, bf16[256,256]{1,0:T(8,128)(2,1)}, f32[]{:T(128)}, /*index=5*/f32[1,256]{1,0:T(1,128)S(1)}, ...), branch_computations={%region_18.19_spmd, %region_19.20_spmd} | conditional | flops 101646592 | bytes 10623094 | solution.py:69
  446.0 5.4 copy.29
  454.1 1.7 fusion.198
  455.8 10.6 %conditional.25 = (f32[256,256]{1,0:T(8,128)S(1)}, f32[1,256,256]{2,1,0:T(8,128)S(1)}) conditional(s32[]{:T(128)} %convert_element_type.215, () %tuple.279, (s32[1,1,16,256,256]{4,3,2,1,0:T(8,128)}, s32[]{:T(128)}, bf16[16,256,256]{2,1,0:T(8,128)(2,1)}, bf16[256,256]{1,0:T(8,128)(2,1)}, f32[]{:T(128)}, /*index=5*/f32[1,256]{1,0:T(1,128)S(1)}, ...), branch_computations={%region_20.21_spmd, %region_21.22_spmd} | conditional | flops 101646592 | bytes 10623094 | solution.py:69
  458.3 5.4 copy.30
  466.4 1.7 fusion.197
  468.2 10.5 %conditional.26 = (f32[256,256]{1,0:T(8,128)S(1)}, f32[1,256,256]{2,1,0:T(8,128)S(1)}) conditional(s32[]{:T(128)} %convert_element_type.216, () %tuple.281, (s32[1,1,16,256,256]{4,3,2,1,0:T(8,128)}, s32[]{:T(128)}, bf16[16,256,256]{2,1,0:T(8,128)(2,1)}, bf16[256,256]{1,0:T(8,128)(2,1)}, f32[]{:T(128)}, /*index=5*/f32[1,256]{1,0:T(1,128)S(1)}, ...), branch_computations={%region_22.23_spmd, %region_23.24_spmd} | conditional | flops 101646592 | bytes 10623094 | solution.py:69
  470.5 5.4 copy.31
  478.6 1.7 fusion.196
  480.3 10.9 %conditional.27 = (f32[256,256]{1,0:T(8,128)S(1)}, f32[1,256,256]{2,1,0:T(8,128)S(1)}) conditional(s32[]{:T(128)} %convert_element_type.217, () %tuple.283, (s32[1,1,16,256,256]{4,3,2,1,0:T(8,128)}, s32[]{:T(128)}, bf16[16,256,256]{2,1,0:T(8,128)(2,1)}, bf16[256,256]{1,0:T(8,128)(2,1)}, f32[]{:T(128)}, /*index=5*/f32[1,256]{1,0:T(1,128)S(1)}, ...), branch_computations={%region_24.25_spmd, %region_25.26_spmd} | conditional | flops 101646592 | bytes 10623094 | solution.py:69
  483.1 5.4 copy.32
  491.3 1.7 fusion.195
  493.0 12.3 %conditional.28 = (f32[256,256]{1,0:T(8,128)S(1)}, f32[1,256,256]{2,1,0:T(8,128)}) conditional(s32[]{:T(128)} %convert_element_type.218, () %tuple.285, (s32[1,1,16,256,256]{4,3,2,1,0:T(8,128)}, s32[]{:T(128)}, bf16[16,256,256]{2,1,0:T(8,128)(2,1)}, bf16[256,256]{1,0:T(8,128)(2,1)}, f32[]{:T(128)}, /*index=5*/f32[1,256]{1,0:T(1,128)S(1)}, ...), branch_computations={%region_26.27_spmd, %region_27.28_spmd} | conditional | flops 101646592 | bytes 10623094 | solution.py:69
  496.4 5.4 copy.33
  505.3 1.9 fusion.205
  507.1 13.3 %conditional.29 = (f32[256,256]{1,0:T(8,128)}, f32[1,256,256]{2,1,0:T(8,128)}) conditional(s32[]{:T(128)} %convert_element_type.219, () %tuple.287, (s32[1,1,16,256,256]{4,3,2,1,0:T(8,128)}, s32[]{:T(128)}, bf16[16,256,256]{2,1,0:T(8,128)(2,1)}, bf16[256,256]{1,0:T(8,128)(2,1)}, f32[]{:T(128)}, /*index=5*/f32[1,256]{1,0:T(1,128)S(1)}, ...), branch_computations={%region_28.29_spmd, %region_29.30_spmd} | conditional | flops 101646592 | bytes 10623094 | solution.py:69
  511.0 5.4 copy.34
  518.6 1.8 fusion.161
  520.5 13.3 %conditional.30 = (f32[256,256]{1,0:T(8,128)}, f32[1,256,256]{2,1,0:T(8,128)}) conditional(s32[]{:T(128)} %convert_element_type.220, () %tuple.289, (s32[1,1,16,256,256]{4,3,2,1,0:T(8,128)}, s32[]{:T(128)}, bf16[16,256,256]{2,1,0:T(8,128)(2,1)}, bf16[256,256]{1,0:T(8,128)(2,1)}, f32[]{:T(128)}, /*index=5*/f32[1,256]{1,0:T(1,128)S(1)}, ...), branch_computations={%region_30.31_spmd, %region_31.32_spmd} | conditional | flops 101646592 | bytes 10623094 | solution.py:69
  524.3 5.4 copy.35
  531.9 1.9 fusion.173
  533.8 11.7 %conditional.31 = (f32[256,256]{1,0:T(8,128)S(1)}, f32[1,256,256]{2,1,0:T(8,128)S(1)}) conditional(s32[]{:T(128)} %convert_element_type.221, () %tuple.291, (s32[1,1,16,256,256]{4,3,2,1,0:T(8,128)}, s32[]{:T(128)}, bf16[16,256,256]{2,1,0:T(8,128)(2,1)}, bf16[256,256]{1,0:T(8,128)(2,1)}, f32[]{:T(128)}, /*index=5*/f32[1,256]{1,0:T(1,128)S(1)}, ...), branch_computations={%region_32.33_spmd, %region_33.34_spmd} | conditional | flops 101646592 | bytes 10627218 | solution.py:69
  537.4 5.4 copy.36
  546.3 2.8 slice_bitcast_fusion.11
  550.7 11.3 %select_add_fusion = f32[16,256,256]{2,1,0:T(8,128)} fusion(f32[256,256]{1,0:T(8,128)S(1)} %add_add_fusion, f32[256,256]{1,0:T(8,128)S(1)} %get-tuple-element.1640, f32[256,256]{1,0:T(8,128)S(1)} %get-tuple-element.1641, f32[256,256]{1,0:T(8,128)S(1)} %get-tuple-element.1642, f32[256,256]{1,0:T(8,128)S(1)} %copy-done.20, ...), kind=kLoop, calls=%fused_computation.288 | loop fusion | flops 34603008 | bytes 8651024 | tf_op jit(solution)/shard_map/add | solution.py:78
  562.1 109.4 %reduce-scatter.2.cloned.1.call-done = f32[1,256,256]{2,1,0:T(8,128)} async-done(((f32[16,256,256]{2,1,0:T(8,128)}), f32[1,256,256]{2,1,0:T(8,128)}) %reduce-scatter.2.cloned.1.call-update) | async-done | bytes 262160 | tf_op jit(solution)/shard_map/reduce_scatter | solution.py:79
  671.6 192.9 %all-gather.6.cloned.1.call-done = f32[32,256,256]{2,1,0:T(8,128)} async-done(((f32[1,256,256]{2,1,0:T(8,128)}), f32[32,256,256]{2,1,0:T(8,128)}) %all-gather.6.cloned.1.call-update) | async-done | bytes 8388624 | tf_op jit(solution)/shard_map/all_gather | solution.py:35
  864.5 4.6 reduce.33
  (152 shorter events, 53.6 us)
Async XLA Ops:
  6.5 259.4 %all-reduce.3.cloned.1.call-start = ((), (), s32[]{:S(2)}) async-start(), calls=%async_computation.2 | async-start | bytes 262144 | tf_op jit(solution)/shard_map/psum | solution.py:12
  89.5 0.8 copy-start.16
  90.3 254.8 %all-gather.4.cloned.1.call-start = ((), (), s32[]{:S(2)}) async-start(), calls=%async_computation.1 | async-start | bytes 2228224 | tf_op jit(solution)/shard_map/all_gather | solution.py:53
  91.0 580.5 %reduce-scatter.2.cloned.1.call-start = ((), (), s32[]{:S(2)}) async-start(), calls=%async_computation.3 | async-start | bytes 4456448 | tf_op jit(solution)/shard_map/reduce_scatter | solution.py:79
  115.1 365.3 %copy-start.21 = (f32[16,256]{1,0:T(8,128)}, f32[16,256]{1,0:T(8,128)S(1)}, u32[]{:S(2)}) copy-start(f32[16,256]{1,0:T(8,128)S(1)} %reshape.990) | copy-start | bytes 49156
  347.8 5.4 copy-start
  360.9 5.4 copy-start.1
  372.5 5.4 copy-start.2
  384.9 5.4 copy-start.3
  397.2 5.4 copy-start.4
  409.3 5.4 copy-start.5
  421.4 5.4 copy-start.6
  433.5 5.4 copy-start.7
  446.0 5.4 copy-start.8
  458.3 5.4 copy-start.9
  470.5 5.4 copy-start.10
  483.1 5.4 copy-start.11
  496.4 5.4 copy-start.12
  511.0 5.4 copy-start.13
  524.2 5.4 copy-start.14
  537.3 5.5 copy-start.15
  537.3 5.5 copy-start.35
  545.5 0.7 copy-start.17
  545.5 0.8 copy-start.19
  546.3 3.0 copy-start.18
  549.1 1.5 copy-start.20
  549.1 1.5 copy-start.22
  549.1 1.5 copy-start.23
  549.1 1.5 copy-start.24
  549.2 1.5 copy-start.25
  549.2 1.5 copy-start.26
  549.2 1.5 copy-start.27
  549.2 1.5 copy-start.28
  549.2 1.5 copy-start.29
  549.2 1.5 copy-start.30
  549.2 1.5 copy-start.31
  549.2 1.5 copy-start.32
  549.2 1.5 copy-start.33
  549.2 1.5 copy-start.34
  549.3 1.5 copy-start.36
  562.1 302.4 %all-gather.6.cloned.1.call-start = ((), (), s32[]{:S(2)}) async-start(), calls=%async_computation.4 | async-start | bytes 8650752 | tf_op jit(solution)/shard_map/all_gather | solution.py:35
Sparse Core Ops, SparseCore 0:
  90.4 175.4 all-reduce.2
  269.2 75.8 all-gather.3
  562.2 109.3 reduce-scatter.1
  673.5 190.9 all-gather.5
